TPU v7x, 32 devices: a whole 2x2x4 slice. The times are simulated.
32 devices in a mesh: groups: 2 (over y), genome: 4 (over z), ancestry: 2 (over x), trait: 2 (over core).
Axes of the slice: x: 2, y: 2, z: 4, core: 2. Of those that a mesh axis runs over, the one named last changes fastest.
Arguments:
- zscores: float32 [2, 64, 8192], P('ancestry', 'trait', ('groups', 'genome')), parts along dimension 2
- ld_diag: bfloat16 [2, 8192, 1024], P('ancestry', ('groups', 'genome')), parts along dimension 1, as said below
- ld_next: bfloat16 [2, 8192, 1024], P('ancestry', ('groups', 'genome')), parts along dimension 1
- prior_precision: float32 [2, 2], replicated, as said below
- chrom_cut: int32 [8], P('groups'), parts along dimension 0, may hold values from 0 to 2047
- band_width: int32 [8], P('groups'), parts along dimension 0, may hold values from 512 to 2047
Outputs:
- effect_sizes: float32 [2, 64, 8192], P('ancestry', 'trait', ('groups', 'genome')), parts along dimension 2
There are 2 independent parts, one for each index of `groups`. A program takes and returns all parts, laid end to end along the dimension named above; an argument that names none is the same for every part. Nothing has to cross between parts.
Inputs may be any that keep to these rules, and one draw needn't show every extreme that they name: `chrom_cut`: an entry below 1024 is the offset within its block of the first variant of a new chromosome; 1024 or more means the block holds no chromosome start. `band_width`: LD between two variants counts only when their distance is below the smaller width of their two blocks. `ld_diag`: each 1024 x 1024 diagonal block is symmetric with a positive diagonal. `prior_precision`: symmetric; each diagonal entry exceeds the sum of the magnitudes of the other entries of its row.
All inputs are finite; a program needn't handle non-finite values.
Results may differ from a plain program's by a relative error of at most 0.0025.
Values may be sent and summed in bfloat16 or wider, within the bound.
A program may use at most 64 MiB of HBM per device.

v0:
```python
import jax
import jax.numpy as jnp
from jax import lax
from jax.sharding import PartitionSpec as P

ITERS = 3


def passed_along(value, axis, steps):
    count = lax.axis_size(axis)
    leading, last = (max(0, -steps), min(count, count - steps))
    return lax.ppermute(value, axis, [(source, source + steps) for source in range(leading, last)])


def block_masks(block_len, cut_here, cut_after, width_here, width_after):
    row_ids = jnp.arange(block_len, dtype=jnp.int32)[:, None]
    col_ids = jnp.arange(block_len, dtype=jnp.int32)[None, :]
    opened = cut_here < block_len
    same_chrom = opened & (row_ids >= cut_here) == opened & (col_ids >= cut_here)
    inside = (jnp.abs(row_ids - col_ids) < width_here) & same_chrom
    before_cut = opened & (row_ids < cut_here)
    across = (
        (block_len + col_ids - row_ids < jnp.minimum(width_here, width_after))
        & jnp.logical_not(before_cut)
        & (col_ids < cut_after)
    )
    return (inside, across)


def curvature_sum(direction, image_vec):
    return lax.psum(jnp.sum(direction * image_vec, axis=1), ("genome", "ancestry"))


def residual_norm(residual, precond):
    return lax.psum(jnp.sum(residual * precond, axis=1), ("genome", "ancestry"))


def body(zscores, ld_diag, ld_next, prior_precision, chrom_cut, band_width):
    block_len = ld_diag.shape[1]
    block_count = lax.axis_size("genome")
    position = lax.axis_index("genome")
    ancestry_id = lax.axis_index("ancestry")
    following = jnp.minimum(position + 1, block_count - 1)
    inside, across = block_masks(
        block_len,
        chrom_cut[position],
        chrom_cut[following],
        band_width[position],
        band_width[following],
    )
    zero_value = jnp.zeros((), jnp.bfloat16)
    diag_tile = jnp.where(inside, ld_diag[0], zero_value)
    next_tile = jnp.where(across, ld_next[0], zero_value)
    prior_row = lax.dynamic_index_in_dim(prior_precision, ancestry_id, 0, keepdims=False)
    self_weight = lax.dynamic_index_in_dim(prior_row, ancestry_id, 0, keepdims=False)
    scaling = 1.0 / (jnp.diagonal(ld_diag[0]).astype(jnp.float32) + self_weight)
    residual = zscores[0]
    solution = jnp.zeros(residual.shape, jnp.float32)
    precond = scaling[None, :] * residual
    direction = precond
    norm_now = residual_norm(residual, precond)
    for iteration in range(ITERS):
        direction_bf = direction.astype(jnp.bfloat16)
        band_out = jnp.dot(direction_bf, diag_tile, preferred_element_type=jnp.float32)
        upper_part = passed_along(direction_bf, "genome", -1)
        band_out = band_out + lax.dot_general(
            upper_part, next_tile, (((1,), (1,)), ((), ())), preferred_element_type=jnp.float32
        )
        carried = jnp.dot(direction_bf, next_tile, preferred_element_type=jnp.float32)
        band_out = band_out + passed_along(carried.astype(jnp.bfloat16), "genome", 1).astype(
            carried.dtype
        )
        coupled = jnp.einsum(
            "b,btv->tv",
            prior_row,
            lax.all_gather(direction_bf[None], "ancestry", axis=0, tiled=True).astype(jnp.float32),
            precision=lax.Precision.HIGHEST,
        )
        image_vec = band_out + coupled
        step_len = norm_now / curvature_sum(direction, image_vec)
        solution = solution + step_len[:, None] * direction
        if iteration + 1 < ITERS:
            residual = residual - step_len[:, None] * image_vec
            precond = scaling[None, :] * residual
            norm_next = residual_norm(residual, precond)
            direction = precond + (norm_next / norm_now)[:, None] * direction
            norm_now = norm_next
    return solution[None]


def solution(mesh):
    return jax.shard_map(
        body,
        mesh=mesh,
        in_specs=(
            P("ancestry", "trait", ("groups", "genome")),
            P("ancestry", ("groups", "genome"), None),
            P("ancestry", ("groups", "genome"), None),
            P(),
            P("groups"),
            P("groups"),
        ),
        out_specs=P("ancestry", "trait", ("groups", "genome")),
        check_vma=False,
    )
```

profile of v0, /device:TPU:0, one launch (start us, length us, event | category | flops | bytes accessed | tf_op | source)
XLA Modules:
  0.0 168.3 jit_solution(2433427531543962618)
XLA Ops:
  0.0 1.4 dynamic_slice.20
  1.4 16.1 %gather_fusion = bf16[1024]{0:T(1024)(128)(2,1)S(1)} fusion(bf16[1024,1024]{1,0:T(8,128)(2,1)} %bitcast.66, s32[1024]{0:T(1024)S(1)} %bitcast.65), kind=kCustom, calls=%fused_computation | custom fusion | bytes 12288 | tf_op jit(solution)/shard_map/jit(diagonal)/cond/branch_0_fun/gather | solution.py:56
  18.3 1.3 collective-permute-start
  23.5 1.2 fusion.27
  24.7 5.6 %collective-permute-start.1 = (bf16[32,1024]{1,0:T(8,128)(2,1)S(1)}, bf16[32,1024]{1,0:T(8,128)(2,1)S(1)}, u32[]{:S(2)}, u32[]{:S(2)}) collective-permute-start(bf16[32,1024]{1,0:T(8,128)(2,1)S(1)} %fusion.27), channel_id=1, source_target_pairs={{0,4},{4,8},{8,12},{1,5},{5,9},{9,13},{2,6},{6,10},{10,14},{3,7},{... | collective-permute-start | bytes 196616 | tf_op jit(solution)/shard_map/ppermute | solution.py:12
  31.0 4.9 %all_gather.9 = bf16[2,32,1024]{2,1,0:T(8,128)(2,1)S(1)} all-gather(bf16[1,32,1024]{2,1,0:T(8,128)(2,1)S(1)} %multiply_convert_fusion.1), channel_id=1, replica_groups=mesh['groups'=2,'genome'=4,'ancestry'=2,'trait'=2] {'ancestry'}, dimensions={0}, use_global_device_ids=true | all-gather | bytes 196608 | tf_op jit(solution)/shard_map/all_gather | solution.py:76
  35.9 1.2 fusion.6
  37.5 1.9 %fusion.14 = f32[32,1024]{1,0:T(8,128)S(1)} fusion(bf16[1,1024,1024]{2,1,0:T(8,128)(2,1)S(1)} %copy-done.1, s32[]{:T(128)} %bitcast.5, pred[1024]{0:T(1024)(128)(4,1)S(1)} %fusion.48, bf16[1,32,1024]{2,1,0:T(8,128)(2,1)S(1)} %multiply_convert_fusion.1), kind=kOutput, calls=%fused_computation.18 | convolution fusion | flops 73400320 | bytes 2294788 | tf_op jit(solution)/shard_map/dot_general | solution.py:64
  39.4 3.1 %fusion.2 = bf16[1024,1024]{1,0:T(8,128)(2,1)} fusion(s32[]{:T(128)} %bitcast.5, pred[1024]{0:T(1024)(128)(4,1)S(1)} %fusion.48, bf16[1,1024,1024]{2,1,0:T(8,128)(2,1)S(1)} %copy-done.1), kind=kLoop, calls=%fused_computation.7 | loop fusion | flops 6291456 | bytes 4195332 | tf_op jit(solution)/shard_map/jit(_where)/select_n | solution.py:52
  43.1 0.9 fusion.34
  44.0 19.9 %all-reduce = (f32[32]{0:T(128)S(1)}, f32[32]{0:T(128)S(1)}) all-reduce(f32[32]{0:T(128)S(1)} %get-tuple-element.6, f32[32]{0:T(128)S(1)} %get-tuple-element.5), channel_id=1, replica_groups=mesh['groups'=2,'genome'=4,'ancestry'=2,'trait'=2] {'genome','ancestry'}, use_global_device_ids=true, to_apply=%region_1.2 | all-reduce | flops 64 | bytes 512 | tf_op jit(solution)/shard_map/psum | solution.py:35
  64.1 17.1 %psum.44 = f32[32]{0:T(128)S(1)} all-reduce(f32[32]{0:T(128)S(1)} %get-tuple-element.13), channel_id=1, replica_groups=mesh['groups'=2,'genome'=4,'ancestry'=2,'trait'=2] {'genome','ancestry'}, use_global_device_ids=true, to_apply=%region_5.6 | all-reduce | flops 32 | bytes 256 | tf_op jit(solution)/shard_map/psum | solution.py:35
  81.8 1.4 collective-permute-start.2
  83.2 5.0 %all-gather = bf16[64,1024]{1,0:T(8,128)(2,1)S(1)} all-gather(bf16[32,1024]{1,0:T(8,128)(2,1)S(1)} %get-tuple-element.11), channel_id=2, replica_groups=mesh['groups'=2,'genome'=4,'ancestry'=2,'trait'=2] {'ancestry'}, dimensions={0}, use_global_device_ids=true | all-gather | bytes 196608 | tf_op jit(solution)/shard_map/all_gather | solution.py:76
  88.2 4.5 %collective-permute-start.3 = (bf16[32,1024]{1,0:T(8,128)(2,1)S(1)}, bf16[32,1024]{1,0:T(8,128)(2,1)S(1)}, u32[]{:S(2)}, u32[]{:S(2)}) collective-permute-start(bf16[32,1024]{1,0:T(8,128)(2,1)S(1)} %convolution_convert_fusion.1), channel_id=1, source_target_pairs={{0,4},{4,8},{8,12},{1,5},{5,9},{9,13},{2,6},{6,10},{10,14},{3,7},{... | collective-permute-start | bytes 196616 | tf_op jit(solution)/shard_map/ppermute | solution.py:12
  94.7 0.8 multiply_reduce_fusion
  95.5 19.2 %psum.45 = f32[32]{0:T(128)S(1)} all-reduce(f32[32]{0:T(128)S(1)} %get-tuple-element.20), channel_id=1, replica_groups=mesh['groups'=2,'genome'=4,'ancestry'=2,'trait'=2] {'genome','ancestry'}, use_global_device_ids=true, to_apply=%region_7.8 | all-reduce | flops 32 | bytes 256 | tf_op jit(solution)/shard_map/psum | solution.py:31
  115.0 17.2 %psum.46 = f32[32]{0:T(128)S(1)} all-reduce(f32[32]{0:T(128)S(1)} %fusion.39), channel_id=1, replica_groups=mesh['groups'=2,'genome'=4,'ancestry'=2,'trait'=2] {'genome','ancestry'}, use_global_device_ids=true, to_apply=%region_9.10 | all-reduce | flops 32 | bytes 256 | tf_op jit(solution)/shard_map/psum | solution.py:35
  132.3 2.1 %fusion.58 = f32[32,1024]{1,0:T(8,128)S(1)} fusion(bf16[32,1024]{1,0:T(8,128)(2,1)S(1)} %get-tuple-element.9, bf16[1024,1024]{1,0:T(8,128)(2,1)} %fusion.2), kind=kOutput, calls=%fused_computation.84 | convolution fusion | flops 67108864 | bytes 2293760 | tf_op jit(solution)/shard_map/dot_general | solution.py:64
  134.8 1.3 collective-permute-start.4
  136.1 5.0 %all-gather.1 = bf16[64,1024]{1,0:T(8,128)(2,1)S(1)} all-gather(bf16[32,1024]{1,0:T(8,128)(2,1)S(1)} %get-tuple-element.9), channel_id=3, replica_groups=mesh['groups'=2,'genome'=4,'ancestry'=2,'trait'=2] {'ancestry'}, dimensions={0}, use_global_device_ids=true | all-gather | bytes 196608 | tf_op jit(solution)/shard_map/all_gather | solution.py:76
  141.1 4.5 %collective-permute-start.5 = (bf16[32,1024]{1,0:T(8,128)(2,1)S(1)}, bf16[32,1024]{1,0:T(8,128)(2,1)S(1)}, u32[]{:S(2)}, u32[]{:S(2)}) collective-permute-start(bf16[32,1024]{1,0:T(8,128)(2,1)S(1)} %convolution_convert_fusion), channel_id=1, source_target_pairs={{0,4},{4,8},{8,12},{1,5},{5,9},{9,13},{2,6},{6,10},{10,14},{3,7},{... | collective-permute-start | bytes 196616 | tf_op jit(solution)/shard_map/ppermute | solution.py:12
  146.2 1.3 collective-permute-done.5
  148.4 19.1 %psum.47 = f32[32]{0:T(128)S(1)} all-reduce(f32[32]{0:T(128)S(1)} %fusion.30), channel_id=1, replica_groups=mesh['groups'=2,'genome'=4,'ancestry'=2,'trait'=2] {'genome','ancestry'}, use_global_device_ids=true, to_apply=%region_11.12 | all-reduce | flops 32 | bytes 256 | tf_op jit(solution)/shard_map/psum | solution.py:31
  (47 shorter events, 10.0 us)
Async XLA Ops:
  0.0 18.2 %copy-start.2 = (f32[1,32,1024]{2,1,0:T(8,128)S(1)}, f32[1,32,1024]{2,1,0:T(8,128)}, u32[]{:S(2)}) copy-start(f32[1,32,1024]{2,1,0:T(8,128)} %param.6) | copy-start | bytes 393220
  0.0 19.6 %copy-start.6 = (s32[4]{0:T(128)S(1)}, s32[4]{0:T(128)}, u32[]{:S(2)}) copy-start(s32[4]{0:T(128)} %param.11) | copy-start | bytes 52
  0.0 19.6 %copy-start.5 = (s32[4]{0:T(128)S(1)}, s32[4]{0:T(128)}, u32[]{:S(2)}) copy-start(s32[4]{0:T(128)} %param.10) | copy-start | bytes 52
  0.0 23.5 %copy-start.3 = (bf16[1,1024,1024]{2,1,0:T(8,128)(2,1)S(1)}, bf16[1,1024,1024]{2,1,0:T(8,128)(2,1)}, u32[]{:S(2)}) copy-start(bf16[1,1024,1024]{2,1,0:T(8,128)(2,1)} %param.8) | copy-start | bytes 6291460
  18.3 24.8 %collective-permute-start = (bf16[32,1024]{1,0:T(8,128)(2,1)S(1)}, bf16[32,1024]{1,0:T(8,128)(2,1)S(1)}, u32[]{:S(2)}, u32[]{:S(2)}) collective-permute-start(bf16[32,1024]{1,0:T(8,128)(2,1)S(1)} %multiply_convert_fusion), channel_id=1, source_target_pairs={{4,0},{8,4},{12,8},{5,1},{9,5},{13,9},{6,2},{10,6},{14,10},{7,3},{... | collective-permute-start | bytes 196616 | tf_op jit(solution)/shard_map/ppermute | solution.py:12
  23.5 12.4 %copy-start.4 = (bf16[1,1024,1024]{2,1,0:T(8,128)(2,1)S(1)}, bf16[1,1024,1024]{2,1,0:T(8,128)(2,1)}, u32[]{:S(2)}) copy-start(bf16[1,1024,1024]{2,1,0:T(8,128)(2,1)} %param.8) | copy-start | bytes 6291460
  24.7 18.4 %collective-permute-start.1 = (bf16[32,1024]{1,0:T(8,128)(2,1)S(1)}, bf16[32,1024]{1,0:T(8,128)(2,1)S(1)}, u32[]{:S(2)}, u32[]{:S(2)}) collective-permute-start(bf16[32,1024]{1,0:T(8,128)(2,1)S(1)} %fusion.27), channel_id=1, source_target_pairs={{0,4},{4,8},{8,12},{1,5},{5,9},{9,13},{2,6},{6,10},{10,14},{3,7},{... | collective-permute-start | bytes 196616 | tf_op jit(solution)/shard_map/ppermute | solution.py:12
  35.9 1.6 copy-start.1
  39.4 3.1 %copy-start.7 = (f32[2,2]{1,0:T(2,128)S(1)}, f32[2,2]{1,0:T(2,128)}, u32[]{:S(2)}) copy-start(f32[2,2]{1,0:T(2,128)} %param.9) | copy-start | bytes 52
  81.2 11.6 %copy-start = (bf16[1024,1024]{1,0:T(8,128)(2,1)S(1)}, bf16[1024,1024]{1,0:T(8,128)(2,1)}, u32[]{:S(2)}) copy-start(bf16[1024,1024]{1,0:T(8,128)(2,1)} %fusion.2) | copy-start | bytes 6291460
  81.8 12.9 %collective-permute-start.2 = (bf16[32,1024]{1,0:T(8,128)(2,1)S(1)}, bf16[32,1024]{1,0:T(8,128)(2,1)S(1)}, u32[]{:S(2)}, u32[]{:S(2)}) collective-permute-start(bf16[32,1024]{1,0:T(8,128)(2,1)S(1)} %get-tuple-element.11), channel_id=1, source_target_pairs={{4,0},{8,4},{12,8},{5,1},{9,5},{13,9},{6,2},{10,6},{14,10},{7,3},{... | collective-permute-start | bytes 196616 | tf_op jit(solution)/shard_map/ppermute | solution.py:12
  88.2 6.4 %collective-permute-start.3 = (bf16[32,1024]{1,0:T(8,128)(2,1)S(1)}, bf16[32,1024]{1,0:T(8,128)(2,1)S(1)}, u32[]{:S(2)}, u32[]{:S(2)}) collective-permute-start(bf16[32,1024]{1,0:T(8,128)(2,1)S(1)} %convolution_convert_fusion.1), channel_id=1, source_target_pairs={{0,4},{4,8},{8,12},{1,5},{5,9},{9,13},{2,6},{6,10},{10,14},{3,7},{... | collective-permute-start | bytes 196616 | tf_op jit(solution)/shard_map/ppermute | solution.py:12
  134.8 12.7 %collective-permute-start.4 = (bf16[32,1024]{1,0:T(8,128)(2,1)S(1)}, bf16[32,1024]{1,0:T(8,128)(2,1)S(1)}, u32[]{:S(2)}, u32[]{:S(2)}) collective-permute-start(bf16[32,1024]{1,0:T(8,128)(2,1)S(1)} %get-tuple-element.9), channel_id=1, source_target_pairs={{4,0},{8,4},{12,8},{5,1},{9,5},{13,9},{6,2},{10,6},{14,10},{7,3},{... | collective-permute-start | bytes 196616 | tf_op jit(solution)/shard_map/ppermute | solution.py:12
  141.1 6.4 %collective-permute-start.5 = (bf16[32,1024]{1,0:T(8,128)(2,1)S(1)}, bf16[32,1024]{1,0:T(8,128)(2,1)S(1)}, u32[]{:S(2)}, u32[]{:S(2)}) collective-permute-start(bf16[32,1024]{1,0:T(8,128)(2,1)S(1)} %convolution_convert_fusion), channel_id=1, source_target_pairs={{0,4},{4,8},{8,12},{1,5},{5,9},{9,13},{2,6},{6,10},{10,14},{3,7},{... | collective-permute-start | bytes 196616 | tf_op jit(solution)/shard_map/ppermute | solution.py:12
where the time goes:
time: 169 us; the launch traced here: 168 us
  blocking collectives  108 us (64%)
  local copies, waits for them, and re-layouts  18.6 us (11%)
  starting transfers between devices  18.6 us (11%)
  matrix products  10.7 us (6%)
  other arithmetic  8.43 us (5%)
  waiting for transfers between devices  2.16 us (1%)
  between operations  2.13 us (1%)
    psum x3, blocking collectives, residual_norm(): return lax.psum(jnp.sum(residual * precond, axis=1), ('genome', 'ancestry'))  54.3 us
    psum x2, blocking collectives, curvature_sum(): lax.psum(jnp.sum(direction * image_vec, axis=1), ('genome', 'ancestry'))  38.4 us
    ppermute x6, starting transfers between devices, passed_along(): lax.ppermute(value, axis, [(source, source + steps) for source in range(l...  18.6 us
    gather x1, local copies, waits for them, and re-layouts, body(): scaling = 1.0 / (jnp.diagonal(ld_diag[0]).astype(jnp.float32) + self_weight)  16.1 us
    all_gather x3, blocking collectives, body(): lax.all_gather(direction_bf[None], 'ancestry', axis=0, tiled=True)  14.9 us
    dot_general x3, matrix products, body(): jnp.dot(direction_bf, diag_tile, preferred_element_type=jnp.float32)  4.38 us
  transfers between devices with their start and end apart: 6, of which 2 were waited for; matrix products, arithmetic and copies ran while one was open for 7% of the time, Pallas kernels for 0%

commit v1 on v0

v1 whole, which is shorter than its diff:
```python
import functools

import jax
import jax.numpy as jnp
from jax import lax
from jax.experimental import pallas as pl
from jax.experimental.pallas import tpu as pltpu
from jax.sharding import PartitionSpec as P

MESH = pl.DeviceIdType.MESH
COLS = 256
ROWS = 32
LANES = 128
UNROLL_PEERS = 16


def for_each(start, stop, step_fn):
    if stop - start <= UNROLL_PEERS:
        for index in range(start, stop):
            step_fn(index)
    else:
        lax.fori_loop(start, stop, lambda index, carry: (step_fn(index), carry)[1], 0)


def kernel(
    blocks, pops,
    prior, cuts, widths, z_hbm, diag_hbm, next_hbm,
    out_ref,
    zv, dv, nv, scale, p, pb, image, up, anc, carry_out, carry_in, sums, tail,
    load_sem, up_send, up_recv, anc_send, anc_recv, carry_send, carry_recv,
    sums_send, sums_recv, tail_send, tail_recv,
):
    traits, length = zv.shape
    members = blocks * pops
    pos = lax.axis_index("genome")
    pop = lax.axis_index("ancestry")
    before = jnp.maximum(pos - 1, 0)
    after = jnp.minimum(pos + 1, blocks - 1)

    loads = [
        pltpu.make_async_copy(src, dst, load_sem.at[i])
        for i, (src, dst) in enumerate(
            [(z_hbm.at[0], zv), (diag_hbm.at[0], dv), (next_hbm.at[0], nv)]
        )
    ]
    for load in loads:
        load.start()

    def peer(offset):
        return {
            "genome": lax.rem(pos + offset // pops, blocks),
            "ancestry": lax.rem(pop + offset % pops, pops),
        }

    barrier = pltpu.get_barrier_semaphore()
    for_each(
        1, members,
        lambda k: pl.semaphore_signal(barrier, inc=1, device_id=peer(k), device_id_type=MESH),
    )

    def up_copy(k):
        return pltpu.make_async_remote_copy(
            pb.at[k], up.at[k], up_send.at[k], up_recv.at[k],
            device_id={"genome": before}, device_id_type=MESH,
        )

    def carry_copy(k):
        return pltpu.make_async_remote_copy(
            carry_out.at[k], carry_in.at[k], carry_send.at[k], carry_recv.at[k],
            device_id={"genome": after}, device_id_type=MESH,
        )

    def anc_copy(k, shift):
        return pltpu.make_async_remote_copy(
            pb.at[k], anc.at[k, shift - 1], anc_send.at[k, shift - 1], anc_recv.at[k, shift - 1],
            device_id={"ancestry": lax.rem(pop + shift, pops)}, device_id_type=MESH,
        )

    def sums_copy(k):
        return pltpu.make_async_remote_copy(
            sums.at[0], sums.at[k], sums_send.at[k], sums_recv.at[k],
            device_id=peer(k), device_id_type=MESH,
        )

    def tail_copy(k):
        return pltpu.make_async_remote_copy(
            tail.at[0], tail.at[k], tail_send.at[k], tail_recv.at[k],
            device_id=peer(k), device_id_type=MESH,
        )

    has_before = pos > 0
    has_after = pos < blocks - 1

    @pl.when(pos == blocks - 1)
    def _():
        up[...] = jnp.zeros_like(up)

    @pl.when(pos == 0)
    def _():
        carry_in[...] = jnp.zeros_like(carry_in)

    def send_direction(k):
        @pl.when(has_before)
        def _():
            up_copy(k).start()

        for shift in range(1, pops):
            anc_copy(k, shift).start()

    cut_here, cut_after = cuts[pos], cuts[after]
    width_here = widths[pos]
    width_both = jnp.minimum(width_here, widths[after])
    cut_here = jnp.minimum(cut_here, length)
    cut_after = jnp.where(has_after, jnp.minimum(cut_after, length), 0)

    loads[0].wait()
    loads[1].wait()
    self_weight = prior[pop, pop]
    eye = lax.broadcasted_iota(jnp.int32, (LANES, LANES), 0) == lax.broadcasted_iota(
        jnp.int32, (LANES, LANES), 1
    )
    for b in range(length // LANES):
        at = pl.ds(b * LANES, LANES)
        tile = jnp.where(eye, dv[at, at].astype(jnp.float32), 0.0)
        scale[:, at] = 1.0 / (jnp.sum(tile, axis=0, keepdims=True) + self_weight)
    p[0] = scale[...] * zv[...]
    pb[0] = p[0].astype(jnp.bfloat16)

    pl.semaphore_wait(barrier, members - 1)
    send_direction(0)

    col_ids = lax.broadcasted_iota(jnp.int32, (ROWS, length), 1)
    row_base = lax.broadcasted_iota(jnp.int32, (ROWS, 1), 0)

    loads[2].wait()

    def mask_next(i, carry):
        at = pl.ds(pl.multiple_of(i * ROWS, ROWS), ROWS)
        rows = row_base + i * ROWS
        opened = (rows < cut_here) & (cut_here < length)
        high = jnp.minimum(width_both - length + rows, cut_after)
        high = jnp.where(opened, 0, high)
        tile = nv[at, :].astype(jnp.float32)
        nv[at, :] = jnp.where(col_ids < high, tile, 0.0).astype(jnp.bfloat16)
        return carry

    lax.fori_loop(0, length // ROWS, mask_next, 0)

    def send_carry(k):
        for j in range(length // COLS):
            at = pl.ds(j * COLS, COLS)
            carry_out[k, :, at] = jnp.dot(
                pb[k], nv[:, at], preferred_element_type=jnp.float32
            ).astype(jnp.bfloat16)

        @pl.when(has_after)
        def _():
            carry_copy(k).start()

    send_carry(0)

    def mask_diag(i, carry):
        at = pl.ds(pl.multiple_of(i * ROWS, ROWS), ROWS)
        rows = row_base + i * ROWS
        left = rows < cut_here
        low = jnp.maximum(rows - width_here + 1, jnp.where(left, 0, cut_here))
        high = jnp.minimum(rows + width_here, jnp.where(left, cut_here, length))
        tile = dv[at, :].astype(jnp.float32)
        keep = (col_ids >= low) & (col_ids < high)
        dv[at, :] = jnp.where(keep, tile, 0.0).astype(jnp.bfloat16)
        return carry

    lax.fori_loop(0, length // ROWS, mask_diag, 0)

    def dot_diag(k):
        for j in range(length // COLS):
            at = pl.ds(j * COLS, COLS)
            image[k, :, at] = self_weight * pb[k, :, at].astype(jnp.float32) + jnp.dot(
                pb[k], dv[:, at], preferred_element_type=jnp.float32
            )

    def wait_up(k):
        @pl.when(has_after)
        def _():
            up_copy(k).wait_recv()

    def dot_up(k, j):
        at = pl.ds(j * COLS, COLS)
        return lax.dot_general(
            up[k], nv[at, :], (((1,), (1,)), ((), ())), preferred_element_type=jnp.float32
        )

    def coupled(k):
        total = 0.0
        for shift in range(1, pops):
            anc_copy(k, shift).wait_recv()
            other = lax.rem(pop + pops - shift, pops)
            total = total + prior[pop, other] * anc[k, shift - 1].astype(jnp.float32)
        return total

    def inner(left, right):
        return jnp.sum(left * right, axis=1, keepdims=True)

    for k in range(2):
        if k > 0:
            send_direction(k)
            send_carry(k)
        dot_diag(k)
        wait_up(k)
        for j in range(length // COLS):
            at = pl.ds(j * COLS, COLS)
            image[k, :, at] = image[k, :, at] + dot_up(k, j)
        both = image[k] + coupled(k)

        @pl.when(has_before)
        def _():
            carry_copy(k).wait_recv()

        both = both + carry_in[k].astype(jnp.float32)
        image[k] = both
        following = scale[...] * both - p[k]
        p[k + 1] = following
        pb[k + 1] = following.astype(jnp.bfloat16)

    send_direction(2)

    lane_ids = lax.broadcasted_iota(jnp.int32, (traits, LANES), 1)

    def as_rows(columns):
        packed = jnp.zeros((traits, LANES), jnp.float32)
        for j, column in enumerate(columns):
            packed = jnp.where(lane_ids == j, column, packed)
        packed = jnp.concatenate(
            [packed, jnp.zeros((LANES - traits, LANES), jnp.float32)], axis=0
        )
        return jnp.transpose(packed)[:8]

    sums[0] = as_rows([
        inner(p[0], zv[...]), inner(p[1], zv[...]), inner(p[2], zv[...]),
        inner(p[0], image[0]), inner(p[0], image[1]), inner(p[1], image[1]),
        inner(p[2], image[0]), inner(p[2], image[1]),
    ])
    for_each(1, members, lambda k: sums_copy(k).start())

    dot_diag(2)
    wait_up(2)
    for j in range(length // COLS):
        at = pl.ds(j * COLS, COLS)
        image[2, :, at] = image[2, :, at] + 2.0 * dot_up(2, j)
    last = inner(p[2], image[2] + coupled(2))
    tail[0] = as_rows([last])[:1]
    for_each(1, members, lambda k: tail_copy(k).start())

    for_each(1, members, lambda k: sums_copy(k).wait_recv())
    total = jnp.sum(sums[...], axis=0)
    b0, b1, b2, g00, g01, g11, g02, g12 = (total[j : j + 1] for j in range(8))
    l10 = g01 / g00
    d1 = g11 - l10 * g01
    l20 = g02 / g00
    cross = g12 - l20 * g01
    l21 = cross / d1
    y1 = b1 - l10 * b0
    y2 = b2 - l20 * b0 - l21 * y1
    known = l20 * g02 + l21 * cross
    z0 = b0 / g00
    z1 = y1 / d1

    for_each(1, members, lambda k: tail_copy(k).wait_recv())
    g22 = jnp.sum(tail[...], axis=0)
    c2 = y2 / (g22 - known)
    c1 = z1 - l21 * c2
    c0 = z0 - l10 * c1 - l20 * c2
    stacked = jnp.concatenate(
        [c0, c1, c2, jnp.zeros((LANES - 3, LANES), jnp.float32)], axis=0
    )
    stacked = jnp.transpose(stacked)[:traits]
    out_ref[0] = (
        stacked[:, 0:1] * p[0] + stacked[:, 1:2] * p[1] + stacked[:, 2:3] * p[2]
    )

    for k in range(3):
        @pl.when(has_before)
        def _():
            up_copy(k).wait_send()

        for shift in range(1, pops):
            anc_copy(k, shift).wait_send()
    for k in range(2):
        @pl.when(has_after)
        def _():
            carry_copy(k).wait_send()
    for_each(1, members, lambda k: sums_copy(k).wait_send())
    for_each(1, members, lambda k: tail_copy(k).wait_send())


def solution(mesh):
    blocks, pops = mesh.shape["genome"], mesh.shape["ancestry"]
    members = blocks * pops

    def body(zscores, ld_diag, ld_next, prior_precision, chrom_cut, band_width):
        _, traits, length = zscores.shape
        bf16, f32 = jnp.bfloat16, jnp.float32
        dma = pltpu.SemaphoreType.DMA
        others = max(pops - 1, 1)
        return pl.pallas_call(
            functools.partial(kernel, blocks, pops),
            out_shape=jax.ShapeDtypeStruct(zscores.shape, f32),
            in_specs=[pl.BlockSpec(memory_space=pltpu.SMEM)] * 3
            + [pl.BlockSpec(memory_space=pl.ANY)] * 3,
            out_specs=pl.BlockSpec(memory_space=pltpu.VMEM),
            scratch_shapes=[
                pltpu.VMEM((traits, length), f32),
                pltpu.VMEM((length, length), bf16),
                pltpu.VMEM((length, length), bf16),
                pltpu.VMEM((1, length), f32),
                pltpu.VMEM((3, traits, length), f32),
                pltpu.VMEM((3, traits, length), bf16),
                pltpu.VMEM((3, traits, length), f32),
                pltpu.VMEM((3, traits, length), bf16),
                pltpu.VMEM((3, others, traits, length), bf16),
                pltpu.VMEM((2, traits, length), bf16),
                pltpu.VMEM((2, traits, length), bf16),
                pltpu.VMEM((members, 8, LANES), f32),
                pltpu.VMEM((members, 1, LANES), f32),
                dma((3,)), dma((3,)), dma((3,)),
                dma((3, others)), dma((3, others)),
                dma((2,)), dma((2,)),
                dma((members,)), dma((members,)), dma((members,)), dma((members,)),
            ],
            compiler_params=pltpu.CompilerParams(
                collective_id=0, has_side_effects=True, vmem_limit_bytes=32 << 20
            ),
        )(prior_precision, chrom_cut, band_width, zscores, ld_diag, ld_next)

    return jax.shard_map(
        body,
        mesh=mesh,
        in_specs=(
            P("ancestry", "trait", ("groups", "genome")),
            P("ancestry", ("groups", "genome"), None),
            P("ancestry", ("groups", "genome"), None),
            P(),
            P("groups"),
            P("groups"),
        ),
        out_specs=P("ancestry", "trait", ("groups", "genome")),
        check_vma=False,
    )
```

time: 169 us -> 30 us (0.18)
  blocking collectives: 108 us -> 0 us
  Pallas kernels: 0 us -> 23 us
  starting transfers between devices: 18.6 us -> 0 us
  local copies, waits for them, and re-layouts: 18.6 us -> 6.73 us
  matrix products: 10.7 us -> 0 us
  other arithmetic: 8.43 us -> 0 us
  waiting for transfers between devices: 2.16 us -> 0 us
  between operations: 2.13 us -> 0.02 us
    psum x5 -> x0, blocking collectives: 92.6 us -> none  [the longest x3 54.3 us: residual_norm(): return lax.psum(jnp.sum(residual * precond, axis=1), ('genome', 'ancestry'))]
    pallas_call x0 -> x1, Pallas kernels: none -> 23 us  [body(): pl.pallas_call(functools.partial(kernel, blocks, pops), out_shape=jax.Sha...]
    ppermute x6 -> x0, starting transfers between devices: 18.6 us -> none  [passed_along(): lax.ppermute(value, axis, [(source, source + steps) for source in range(l...]
    gather x1 -> x0, local copies, waits for them, and re-layouts: 16.1 us -> none  [body(): scaling = 1.0 / (jnp.diagonal(ld_diag[0]).astype(jnp.float32) + self_weight)]
    all_gather x3 -> x0, blocking collectives: 14.9 us -> none  [body(): lax.all_gather(direction_bf[None], 'ancestry', axis=0, tiled=True)]
    dot_general x12 -> x0, matrix products: 10.7 us -> none  [the longest x3 4.38 us: body(): jnp.dot(direction_bf, diag_tile, preferred_element_type=jnp.float32)]
    unnamed x16 -> x13, local copies, waits for them, and re-layouts: 0.43 us -> 6.73 us
    select_n x2 -> x0, other arithmetic: 4.32 us -> none  [the longest x1 3.13 us: body(): diag_tile = jnp.where(inside, ld_diag[0], zero_value)]
  transfers between devices with their start and end apart: 6 -> 0, of which waited for: 2 -> 0; matrix products, arithmetic and copies ran while one was open for 7% -> 0% of each run, Pallas kernels for 0% -> 0%
where the time goes in v1:
time: 30 us; the launch traced here: 29.8 us
  Pallas kernels  23 us (77%)
  local copies, waits for them, and re-layouts  6.73 us (22%)
    pallas_call x1, Pallas kernels, body(): pl.pallas_call(functools.partial(kernel, blocks, pops), out_shape=jax.Sha...  23 us
    unnamed x13, local copies, waits for them, and re-layouts  6.73 us

profile of v1, /device:TPU:0, one launch (start us, length us, event | category | flops | bytes accessed | tf_op | source)
XLA Modules:
  0.0 29.8 jit_solution(14324805571241570145)
XLA Ops:
  0.0 0.0 copy-start
  0.0 1.6 %copy-done = bf16[1,1024,1024]{2,1,0:T(8,128)(2,1)S(1)} copy-done((bf16[1,1024,1024]{2,1,0:T(8,128)(2,1)S(1)}, bf16[1,1024,1024]{2,1,0:T(8,128)(2,1)}, u32[]{:S(2)}) %copy-start) | copy-done | bytes 2097176
  1.6 0.0 copy-start.1
  1.6 1.6 %copy-done.1 = bf16[1,1024,1024]{2,1,0:T(8,128)(2,1)S(1)} copy-done((bf16[1,1024,1024]{2,1,0:T(8,128)(2,1)S(1)}, bf16[1,1024,1024]{2,1,0:T(8,128)(2,1)}, u32[]{:S(2)}) %copy-start.1) | copy-done | bytes 2097176
  3.2 0.0 copy-start.2
  3.2 0.9 %copy-done.2 = f32[1,32,1024]{2,1,0:T(8,128)S(1)} copy-done((f32[1,32,1024]{2,1,0:T(8,128)S(1)}, f32[1,32,1024]{2,1,0:T(8,128)}, u32[]{:S(2)}) %copy-start.2) | copy-done | bytes 131096
  4.1 0.0 copy-start.3
  4.1 0.7 %copy-done.3 = f32[2,2]{1,0:T(2,128)S(1)} copy-done((f32[2,2]{1,0:T(2,128)S(1)}, f32[2,2]{1,0:T(2,128)}, u32[]{:S(2)}) %copy-start.3) | copy-done | bytes 40
  4.8 0.0 copy-start.4
  4.8 0.7 %copy-done.4 = s32[4]{0:T(128)S(1)} copy-done((s32[4]{0:T(128)S(1)}, s32[4]{0:T(128)}, u32[]{:S(2)}) %copy-start.4) | copy-done | bytes 40
  5.4 0.0 copy-start.5
  5.4 0.7 %copy-done.5 = s32[4]{0:T(128)S(1)} copy-done((s32[4]{0:T(128)S(1)}, s32[4]{0:T(128)}, u32[]{:S(2)}) %copy-start.5) | copy-done | bytes 40
  6.1 23.0 %shard_map.64 = f32[1,32,1024]{2,1,0:T(8,128)S(1)} custom-call(f32[2,2]{1,0:T(2,128)S(1)} %copy-done.3, s32[4]{0:T(128)S(1)} %copy-done.4, s32[4]{0:T(128)S(1)} %copy-done.5, f32[1,32,1024]{2,1,0:T(8,128)S(1)} %copy-done.2, bf16[1,1024,1024]{2,1,0:T(8,128)(2,1)S(1)} %copy-done, bf16[1,1024,1024]{2,1,0:T(8,128)(2,1)S(1)} %copy-done.1), custom_call_target="tpu_custom_call" | custom-call | tf_op jit(solution)/shard_map/pallas_call | solution.py:305
  29.1 0.7 %copy.8 = f32[1,32,1024]{2,1,0:T(8,128)} copy(f32[1,32,1024]{2,1,0:T(8,128)S(1)} %shard_map.64) | data formatting | bytes 262144
Async XLA Ops:
  0.0 1.6 %copy-start = (bf16[1,1024,1024]{2,1,0:T(8,128)(2,1)S(1)}, bf16[1,1024,1024]{2,1,0:T(8,128)(2,1)}, u32[]{:S(2)}) copy-start(bf16[1,1024,1024]{2,1,0:T(8,128)(2,1)} %diag_hbm.1) | copy-start | bytes 6291460
  1.6 1.6 %copy-start.1 = (bf16[1,1024,1024]{2,1,0:T(8,128)(2,1)S(1)}, bf16[1,1024,1024]{2,1,0:T(8,128)(2,1)}, u32[]{:S(2)}) copy-start(bf16[1,1024,1024]{2,1,0:T(8,128)(2,1)} %next_hbm.1) | copy-start | bytes 6291460
  3.2 0.9 %copy-start.2 = (f32[1,32,1024]{2,1,0:T(8,128)S(1)}, f32[1,32,1024]{2,1,0:T(8,128)}, u32[]{:S(2)}) copy-start(f32[1,32,1024]{2,1,0:T(8,128)} %z_hbm.1) | copy-start | bytes 393220
  4.1 0.7 %copy-start.3 = (f32[2,2]{1,0:T(2,128)S(1)}, f32[2,2]{1,0:T(2,128)}, u32[]{:S(2)}) copy-start(f32[2,2]{1,0:T(2,128)} %prior.1) | copy-start | bytes 52
  4.8 0.7 %copy-start.4 = (s32[4]{0:T(128)S(1)}, s32[4]{0:T(128)}, u32[]{:S(2)}) copy-start(s32[4]{0:T(128)} %cuts.1) | copy-start | bytes 52
  5.4 0.7 %copy-start.5 = (s32[4]{0:T(128)S(1)}, s32[4]{0:T(128)}, u32[]{:S(2)}) copy-start(s32[4]{0:T(128)} %widths.1) | copy-start | bytes 52

commit v2 on v1

--- a/solution.py
+++ b/solution.py
@@ -24,9 +24,9 @@
 
 def kernel(
     blocks, pops,
-    prior, cuts, widths, z_hbm, diag_hbm, next_hbm,
+    prior_hbm, cuts_hbm, widths_hbm, z_hbm, diag_hbm, next_hbm,
     out_ref,
-    zv, dv, nv, scale, p, pb, image, up, anc, carry_out, carry_in, sums, tail,
+    prior, cuts, widths, zv, blocks_on, dv, nv, scale, p, pb, image, up, anc, carry_out, carry_in, sums, tail,
     load_sem, up_send, up_recv, anc_send, anc_recv, carry_send, carry_recv,
     sums_send, sums_recv, tail_send, tail_recv,
 ):
@@ -37,14 +37,24 @@
     before = jnp.maximum(pos - 1, 0)
     after = jnp.minimum(pos + 1, blocks - 1)
 
+    chunks = length // COLS
+    small = [(prior_hbm, prior), (cuts_hbm, cuts), (widths_hbm, widths), (z_hbm.at[0], zv)]
+    for b in range(length // LANES):
+        at = pl.ds(b * LANES, LANES)
+        small.append((diag_hbm.at[0, at, at], blocks_on.at[b]))
+    large = []
+    for src, dst in ((next_hbm, nv), (diag_hbm, dv)):
+        for b in range(chunks):
+            at = pl.ds(b * COLS, COLS)
+            large.append((src.at[0, at], dst.at[at]))
     loads = [
         pltpu.make_async_copy(src, dst, load_sem.at[i])
-        for i, (src, dst) in enumerate(
-            [(z_hbm.at[0], zv), (diag_hbm.at[0], dv), (next_hbm.at[0], nv)]
-        )
+        for i, (src, dst) in enumerate(small + large)
     ]
     for load in loads:
         load.start()
+    next_loads = loads[len(small) : len(small) + chunks]
+    diag_loads = loads[len(small) + chunks :]
 
     def peer(offset):
         return {
@@ -58,21 +68,22 @@
         lambda k: pl.semaphore_signal(barrier, inc=1, device_id=peer(k), device_id_type=MESH),
     )
 
-    def up_copy(k):
-        return pltpu.make_async_remote_copy(
-            pb.at[k], up.at[k], up_send.at[k], up_recv.at[k],
+    def up_copy(k, j):
+        return pltpu.make_async_remote_copy(
+            pb.at[k, j], up.at[k, j], up_send.at[k, j], up_recv.at[k, j],
             device_id={"genome": before}, device_id_type=MESH,
         )
 
-    def carry_copy(k):
-        return pltpu.make_async_remote_copy(
-            carry_out.at[k], carry_in.at[k], carry_send.at[k], carry_recv.at[k],
+    def carry_copy(k, j):
+        return pltpu.make_async_remote_copy(
+            carry_out.at[k, j], carry_in.at[k, j], carry_send.at[k, j], carry_recv.at[k, j],
             device_id={"genome": after}, device_id_type=MESH,
         )
 
-    def anc_copy(k, shift):
-        return pltpu.make_async_remote_copy(
-            pb.at[k], anc.at[k, shift - 1], anc_send.at[k, shift - 1], anc_recv.at[k, shift - 1],
+    def anc_copy(k, j, shift):
+        return pltpu.make_async_remote_copy(
+            pb.at[k, j], anc.at[k, j, shift - 1],
+            anc_send.at[k, j, shift - 1], anc_recv.at[k, j, shift - 1],
             device_id={"ancestry": lax.rem(pop + shift, pops)}, device_id_type=MESH,
         )
 
@@ -99,40 +110,46 @@
     def _():
         carry_in[...] = jnp.zeros_like(carry_in)
 
-    def send_direction(k):
+    def span(j):
+        return pl.ds(j * COLS, COLS)
+
+    def send_direction(k, j):
         @pl.when(has_before)
         def _():
-            up_copy(k).start()
+            up_copy(k, j).start()
 
         for shift in range(1, pops):
-            anc_copy(k, shift).start()
-
+            anc_copy(k, j, shift).start()
+
+    def whole(ref, k):
+        return jnp.concatenate([ref[k, j] for j in range(chunks)], axis=1)
+
+    for load in loads[: len(small)]:
+        load.wait()
     cut_here, cut_after = cuts[pos], cuts[after]
     width_here = widths[pos]
     width_both = jnp.minimum(width_here, widths[after])
     cut_here = jnp.minimum(cut_here, length)
     cut_after = jnp.where(has_after, jnp.minimum(cut_after, length), 0)
 
-    loads[0].wait()
-    loads[1].wait()
     self_weight = prior[pop, pop]
     eye = lax.broadcasted_iota(jnp.int32, (LANES, LANES), 0) == lax.broadcasted_iota(
         jnp.int32, (LANES, LANES), 1
     )
     for b in range(length // LANES):
         at = pl.ds(b * LANES, LANES)
-        tile = jnp.where(eye, dv[at, at].astype(jnp.float32), 0.0)
+        tile = jnp.where(eye, blocks_on[b].astype(jnp.float32), 0.0)
         scale[:, at] = 1.0 / (jnp.sum(tile, axis=0, keepdims=True) + self_weight)
     p[0] = scale[...] * zv[...]
-    pb[0] = p[0].astype(jnp.bfloat16)
+    for j in range(chunks):
+        pb[0, j] = p[0, :, span(j)].astype(jnp.bfloat16)
 
     pl.semaphore_wait(barrier, members - 1)
-    send_direction(0)
+    for j in range(chunks):
+        send_direction(0, j)
 
     col_ids = lax.broadcasted_iota(jnp.int32, (ROWS, length), 1)
     row_base = lax.broadcasted_iota(jnp.int32, (ROWS, 1), 0)
-
-    loads[2].wait()
 
     def mask_next(i, carry):
         at = pl.ds(pl.multiple_of(i * ROWS, ROWS), ROWS)
@@ -144,18 +161,20 @@
         nv[at, :] = jnp.where(col_ids < high, tile, 0.0).astype(jnp.bfloat16)
         return carry
 
-    lax.fori_loop(0, length // ROWS, mask_next, 0)
+    for b in range(chunks):
+        next_loads[b].wait()
+        lax.fori_loop(b * COLS // ROWS, (b + 1) * COLS // ROWS, mask_next, 0)
 
     def send_carry(k):
-        for j in range(length // COLS):
-            at = pl.ds(j * COLS, COLS)
-            carry_out[k, :, at] = jnp.dot(
-                pb[k], nv[:, at], preferred_element_type=jnp.float32
+        direction = whole(pb, k)
+        for j in range(chunks):
+            carry_out[k, j] = jnp.dot(
+                direction, nv[:, span(j)], preferred_element_type=jnp.float32
             ).astype(jnp.bfloat16)
 
-        @pl.when(has_after)
-        def _():
-            carry_copy(k).start()
+            @pl.when(has_after)
+            def _():
+                carry_copy(k, j).start()
 
     send_carry(0)
 
@@ -170,32 +189,37 @@
         dv[at, :] = jnp.where(keep, tile, 0.0).astype(jnp.bfloat16)
         return carry
 
+    for load in diag_loads:
+        load.wait()
     lax.fori_loop(0, length // ROWS, mask_diag, 0)
 
     def dot_diag(k):
-        for j in range(length // COLS):
-            at = pl.ds(j * COLS, COLS)
-            image[k, :, at] = self_weight * pb[k, :, at].astype(jnp.float32) + jnp.dot(
-                pb[k], dv[:, at], preferred_element_type=jnp.float32
+        direction = whole(pb, k)
+        for j in range(chunks):
+            image[k, :, span(j)] = self_weight * pb[k, j].astype(jnp.float32) + jnp.dot(
+                direction, dv[:, span(j)], preferred_element_type=jnp.float32
             )
 
-    def wait_up(k):
-        @pl.when(has_after)
-        def _():
-            up_copy(k).wait_recv()
-
-    def dot_up(k, j):
-        at = pl.ds(j * COLS, COLS)
-        return lax.dot_general(
-            up[k], nv[at, :], (((1,), (1,)), ((), ())), preferred_element_type=jnp.float32
-        )
-
-    def coupled(k):
+    def dot_up(k):
+        total = None
+        for j in range(chunks):
+            @pl.when(has_after)
+            def _():
+                up_copy(k, j).wait_recv()
+
+            part = lax.dot_general(
+                up[k, j], nv[:, span(j)], (((1,), (1,)), ((), ())),
+                preferred_element_type=jnp.float32,
+            )
+            total = part if total is None else total + part
+        return total
+
+    def coupled(k, j):
         total = 0.0
         for shift in range(1, pops):
-            anc_copy(k, shift).wait_recv()
+            anc_copy(k, j, shift).wait_recv()
             other = lax.rem(pop + pops - shift, pops)
-            total = total + prior[pop, other] * anc[k, shift - 1].astype(jnp.float32)
+            total = total + prior[pop, other] * anc[k, j, shift - 1].astype(jnp.float32)
         return total
 
     def inner(left, right):
@@ -203,26 +227,22 @@
 
     for k in range(2):
         if k > 0:
-            send_direction(k)
             send_carry(k)
         dot_diag(k)
-        wait_up(k)
-        for j in range(length // COLS):
-            at = pl.ds(j * COLS, COLS)
-            image[k, :, at] = image[k, :, at] + dot_up(k, j)
-        both = image[k] + coupled(k)
-
-        @pl.when(has_before)
-        def _():
-            carry_copy(k).wait_recv()
-
-        both = both + carry_in[k].astype(jnp.float32)
-        image[k] = both
-        following = scale[...] * both - p[k]
-        p[k + 1] = following
-        pb[k + 1] = following.astype(jnp.bfloat16)
-
-    send_direction(2)
+        image[k] = image[k] + dot_up(k)
+        for j in range(chunks):
+            both = image[k, :, span(j)] + coupled(k, j)
+
+            @pl.when(has_before)
+            def _():
+                carry_copy(k, j).wait_recv()
+
+            both = both + carry_in[k, j].astype(jnp.float32)
+            image[k, :, span(j)] = both
+            following = scale[:, span(j)] * both - p[k, :, span(j)]
+            p[k + 1, :, span(j)] = following
+            pb[k + 1, j] = following.astype(jnp.bfloat16)
+            send_direction(k + 1, j)
 
     lane_ids = lax.broadcasted_iota(jnp.int32, (traits, LANES), 1)
 
@@ -243,11 +263,8 @@
     for_each(1, members, lambda k: sums_copy(k).start())
 
     dot_diag(2)
-    wait_up(2)
-    for j in range(length // COLS):
-        at = pl.ds(j * COLS, COLS)
-        image[2, :, at] = image[2, :, at] + 2.0 * dot_up(2, j)
-    last = inner(p[2], image[2] + coupled(2))
+    other_part = jnp.concatenate([coupled(2, j) for j in range(chunks)], axis=1)
+    last = inner(p[2], image[2] + 2.0 * dot_up(2) + other_part)
     tail[0] = as_rows([last])[:1]
     for_each(1, members, lambda k: tail_copy(k).start())
 
@@ -279,16 +296,18 @@
     )
 
     for k in range(3):
-        @pl.when(has_before)
-        def _():
-            up_copy(k).wait_send()
-
-        for shift in range(1, pops):
-            anc_copy(k, shift).wait_send()
+        for j in range(chunks):
+            @pl.when(has_before)
+            def _():
+                up_copy(k, j).wait_send()
+
+            for shift in range(1, pops):
+                anc_copy(k, j, shift).wait_send()
     for k in range(2):
-        @pl.when(has_after)
-        def _():
-            carry_copy(k).wait_send()
+        for j in range(chunks):
+            @pl.when(has_after)
+            def _():
+                carry_copy(k, j).wait_send()
     for_each(1, members, lambda k: sums_copy(k).wait_send())
     for_each(1, members, lambda k: tail_copy(k).wait_send())
 
@@ -302,33 +321,38 @@
         bf16, f32 = jnp.bfloat16, jnp.float32
         dma = pltpu.SemaphoreType.DMA
         others = max(pops - 1, 1)
+        chunks = length // COLS
         return pl.pallas_call(
             functools.partial(kernel, blocks, pops),
             out_shape=jax.ShapeDtypeStruct(zscores.shape, f32),
-            in_specs=[pl.BlockSpec(memory_space=pltpu.SMEM)] * 3
-            + [pl.BlockSpec(memory_space=pl.ANY)] * 3,
+            in_specs=[pl.BlockSpec(memory_space=pltpu.HBM)] * 6,
             out_specs=pl.BlockSpec(memory_space=pltpu.VMEM),
             scratch_shapes=[
+                pltpu.SMEM(prior_precision.shape, f32),
+                pltpu.SMEM(chrom_cut.shape, jnp.int32),
+                pltpu.SMEM(band_width.shape, jnp.int32),
                 pltpu.VMEM((traits, length), f32),
+                pltpu.VMEM((length // LANES, LANES, LANES), bf16),
                 pltpu.VMEM((length, length), bf16),
                 pltpu.VMEM((length, length), bf16),
                 pltpu.VMEM((1, length), f32),
                 pltpu.VMEM((3, traits, length), f32),
-                pltpu.VMEM((3, traits, length), bf16),
+                pltpu.VMEM((3, chunks, traits, COLS), bf16),
                 pltpu.VMEM((3, traits, length), f32),
-                pltpu.VMEM((3, traits, length), bf16),
-                pltpu.VMEM((3, others, traits, length), bf16),
-                pltpu.VMEM((2, traits, length), bf16),
-                pltpu.VMEM((2, traits, length), bf16),
+                pltpu.VMEM((3, chunks, traits, COLS), bf16),
+                pltpu.VMEM((3, chunks, others, traits, COLS), bf16),
+                pltpu.VMEM((2, chunks, traits, COLS), bf16),
+                pltpu.VMEM((2, chunks, traits, COLS), bf16),
                 pltpu.VMEM((members, 8, LANES), f32),
                 pltpu.VMEM((members, 1, LANES), f32),
-                dma((3,)), dma((3,)), dma((3,)),
-                dma((3, others)), dma((3, others)),
-                dma((2,)), dma((2,)),
+                dma((4 + length // LANES + 2 * chunks,)),
+                dma((3, chunks)), dma((3, chunks)),
+                dma((3, chunks, others)), dma((3, chunks, others)),
+                dma((2, chunks)), dma((2, chunks)),
                 dma((members,)), dma((members,)), dma((members,)), dma((members,)),
             ],
             compiler_params=pltpu.CompilerParams(
-                collective_id=0, has_side_effects=True, vmem_limit_bytes=32 << 20
+                collective_id=0, has_side_effects=True, vmem_limit_bytes=64 << 20
             ),
         )(prior_precision, chrom_cut, band_width, zscores, ld_diag, ld_next)
 

time: 30 us -> 25.1 us (0.84)
  local copies, waits for them, and re-layouts: 6.73 us -> 1.57 us
  Pallas kernels: 23 us -> 23.4 us
    unnamed x13 -> x1, local copies, waits for them, and re-layouts: 6.73 us -> 1.57 us
    pallas_call x1, Pallas kernels: 23 us -> 23.4 us  [body(): pl.pallas_call(functools.partial(kernel, blocks, pops), out_shape=jax.Sha...]
where the time goes in v2:
time: 25.1 us; the launch traced here: 24.9 us
  Pallas kernels  23.4 us (93%)
  local copies, waits for them, and re-layouts  1.57 us (6%)
    pallas_call x1, Pallas kernels, body(): pl.pallas_call(functools.partial(kernel, blocks, pops), out_shape=jax.Sha...  23.4 us
    unnamed x1, local copies, waits for them, and re-layouts  1.57 us

profile of v2, /device:TPU:0, one launch (start us, length us, event | category | flops | bytes accessed | tf_op | source)
XLA Modules:
  0.0 24.9 jit_solution(4320880940046416507)
XLA Ops:
  0.0 23.4 %shard_map.64 = f32[1,32,1024]{2,1,0:T(8,128)} custom-call(f32[2,2]{1,0:T(2,128)} %prior_hbm.1, s32[4]{0:T(128)} %cuts_hbm.1, s32[4]{0:T(128)} %widths_hbm.1, f32[1,32,1024]{2,1,0:T(8,128)} %z_hbm.1, bf16[1,1024,1024]{2,1,0:T(8,128)(2,1)} %diag_hbm.1, bf16[1,1024,1024]{2,1,0:T(8,128)(2,1)} %next_hbm.1), custom_call_target="tpu_custom_call" | custom-call | tf_op jit(solution)/shard_map/pallas_call | solution.py:325
  23.4 1.6 %copy.8 = f32[1,32,1024]{2,1,0:T(8,128)} copy(f32[1,32,1024]{2,1,0:T(8,128)} %shard_map.64) | data formatting | bytes 262144

commit v3 on v2

--- a/solution.py
+++ b/solution.py
@@ -8,8 +8,8 @@
 from jax.sharding import PartitionSpec as P
 
 MESH = pl.DeviceIdType.MESH
-COLS = 256
-ROWS = 32
+COLS = 512
+ROWS = 64
 LANES = 128
 UNROLL_PEERS = 16
 
@@ -26,7 +26,7 @@
     blocks, pops,
     prior_hbm, cuts_hbm, widths_hbm, z_hbm, diag_hbm, next_hbm,
     out_ref,
-    prior, cuts, widths, zv, blocks_on, dv, nv, scale, p, pb, image, up, anc, carry_out, carry_in, sums, tail,
+    prior, cuts, widths, zv, dv, nv, tv, scale, p, pb, image, up, anc, carry_out, carry_in, sums, tail,
     load_sem, up_send, up_recv, anc_send, anc_recv, carry_send, carry_recv,
     sums_send, sums_recv, tail_send, tail_recv,
 ):
@@ -39,11 +39,8 @@
 
     chunks = length // COLS
     small = [(prior_hbm, prior), (cuts_hbm, cuts), (widths_hbm, widths), (z_hbm.at[0], zv)]
-    for b in range(length // LANES):
-        at = pl.ds(b * LANES, LANES)
-        small.append((diag_hbm.at[0, at, at], blocks_on.at[b]))
     large = []
-    for src, dst in ((next_hbm, nv), (diag_hbm, dv)):
+    for src, dst in ((diag_hbm, dv), (next_hbm, nv)):
         for b in range(chunks):
             at = pl.ds(b * COLS, COLS)
             large.append((src.at[0, at], dst.at[at]))
@@ -53,18 +50,27 @@
     ]
     for load in loads:
         load.start()
-    next_loads = loads[len(small) : len(small) + chunks]
-    diag_loads = loads[len(small) + chunks :]
+    next_loads = loads[len(small) + chunks :]
+
+    me = pos * pops + pop
+    late = pos >= blocks // 2
 
     def peer(offset):
+        jump = blocks - 1 - offset // pops
+        jump = jnp.where(late, blocks - jump, jump)
         return {
-            "genome": lax.rem(pos + offset // pops, blocks),
-            "ancestry": lax.rem(pop + offset % pops, pops),
+            "genome": lax.rem(pos + jump, blocks),
+            "ancestry": lax.rem(pop + pops - 1 - offset % pops, pops),
         }
+
+    def sent_by(offset):
+        jump = offset // pops
+        there = lax.rem(pos + jump, blocks) * pops + lax.rem(pop + offset % pops, pops)
+        return there
 
     barrier = pltpu.get_barrier_semaphore()
     for_each(
-        1, members,
+        0, members - 1,
         lambda k: pl.semaphore_signal(barrier, inc=1, device_id=peer(k), device_id_type=MESH),
     )
 
@@ -80,23 +86,29 @@
             device_id={"genome": after}, device_id_type=MESH,
         )
 
-    def anc_copy(k, j, shift):
-        return pltpu.make_async_remote_copy(
-            pb.at[k, j], anc.at[k, j, shift - 1],
-            anc_send.at[k, j, shift - 1], anc_recv.at[k, j, shift - 1],
+    def anc_copy(k, shift):
+        return pltpu.make_async_remote_copy(
+            pb.at[k], anc.at[k, shift - 1], anc_send.at[k, shift - 1], anc_recv.at[k, shift - 1],
             device_id={"ancestry": lax.rem(pop + shift, pops)}, device_id_type=MESH,
         )
 
     def sums_copy(k):
         return pltpu.make_async_remote_copy(
-            sums.at[0], sums.at[k], sums_send.at[k], sums_recv.at[k],
+            sums.at[me], sums.at[me], sums_send.at[k], sums_recv.at[me],
             device_id=peer(k), device_id_type=MESH,
         )
 
     def tail_copy(k):
         return pltpu.make_async_remote_copy(
-            tail.at[0], tail.at[k], tail_send.at[k], tail_recv.at[k],
+            tail.at[me], tail.at[me], tail_send.at[k], tail_recv.at[me],
             device_id=peer(k), device_id_type=MESH,
+        )
+
+    def arrival(ref, send_sem, recv_sem, k):
+        slot = sent_by(k)
+        return pltpu.make_async_remote_copy(
+            ref.at[slot], ref.at[slot], send_sem.at[0], recv_sem.at[slot],
+            device_id=peer(0), device_id_type=MESH,
         )
 
     has_before = pos > 0
@@ -118,13 +130,14 @@
         def _():
             up_copy(k, j).start()
 
-        for shift in range(1, pops):
-            anc_copy(k, j, shift).start()
+        if j == chunks - 1:
+            for shift in range(1, pops):
+                anc_copy(k, shift).start()
 
     def whole(ref, k):
         return jnp.concatenate([ref[k, j] for j in range(chunks)], axis=1)
 
-    for load in loads[: len(small)]:
+    for load in loads[: len(small) + chunks]:
         load.wait()
     cut_here, cut_after = cuts[pos], cuts[after]
     width_here = widths[pos]
@@ -138,7 +151,7 @@
     )
     for b in range(length // LANES):
         at = pl.ds(b * LANES, LANES)
-        tile = jnp.where(eye, blocks_on[b].astype(jnp.float32), 0.0)
+        tile = jnp.where(eye, dv[at, at].astype(jnp.float32), 0.0)
         scale[:, at] = 1.0 / (jnp.sum(tile, axis=0, keepdims=True) + self_weight)
     p[0] = scale[...] * zv[...]
     for j in range(chunks):
@@ -189,8 +202,6 @@
         dv[at, :] = jnp.where(keep, tile, 0.0).astype(jnp.bfloat16)
         return carry
 
-    for load in diag_loads:
-        load.wait()
     lax.fori_loop(0, length // ROWS, mask_diag, 0)
 
     def dot_diag(k):
@@ -207,20 +218,29 @@
             def _():
                 up_copy(k, j).wait_recv()
 
-            part = lax.dot_general(
-                up[k, j], nv[:, span(j)], (((1,), (1,)), ((), ())),
-                preferred_element_type=jnp.float32,
-            )
+            if k == 0:
+                part = lax.dot_general(
+                    up[k, j], nv[:, span(j)], (((1,), (1,)), ((), ())),
+                    preferred_element_type=jnp.float32,
+                )
+            else:
+                part = jnp.dot(up[k, j], tv[span(j)], preferred_element_type=jnp.float32)
             total = part if total is None else total + part
         return total
 
     def coupled(k, j):
         total = 0.0
         for shift in range(1, pops):
-            anc_copy(k, j, shift).wait_recv()
+            if j == 0:
+                anc_copy(k, shift).wait_recv()
             other = lax.rem(pop + pops - shift, pops)
-            total = total + prior[pop, other] * anc[k, j, shift - 1].astype(jnp.float32)
+            total = total + prior[pop, other] * anc[k, shift - 1, j].astype(jnp.float32)
         return total
+
+    def turn_next():
+        for i in range(length // LANES):
+            at = pl.ds(i * LANES, LANES)
+            tv[at] = jnp.transpose(nv[:, at])
 
     def inner(left, right):
         return jnp.sum(left * right, axis=1, keepdims=True)
@@ -229,6 +249,8 @@
         if k > 0:
             send_carry(k)
         dot_diag(k)
+        if k == 1:
+            turn_next()
         image[k] = image[k] + dot_up(k)
         for j in range(chunks):
             both = image[k, :, span(j)] + coupled(k, j)
@@ -255,20 +277,20 @@
         )
         return jnp.transpose(packed)[:8]
 
-    sums[0] = as_rows([
+    sums[me] = as_rows([
         inner(p[0], zv[...]), inner(p[1], zv[...]), inner(p[2], zv[...]),
         inner(p[0], image[0]), inner(p[0], image[1]), inner(p[1], image[1]),
         inner(p[2], image[0]), inner(p[2], image[1]),
     ])
-    for_each(1, members, lambda k: sums_copy(k).start())
+    for_each(0, members - 1, lambda k: sums_copy(k).start())
 
     dot_diag(2)
     other_part = jnp.concatenate([coupled(2, j) for j in range(chunks)], axis=1)
     last = inner(p[2], image[2] + 2.0 * dot_up(2) + other_part)
-    tail[0] = as_rows([last])[:1]
-    for_each(1, members, lambda k: tail_copy(k).start())
-
-    for_each(1, members, lambda k: sums_copy(k).wait_recv())
+    tail[me] = as_rows([last])[:1]
+    for_each(0, members - 1, lambda k: tail_copy(k).start())
+
+    for_each(1, members, lambda k: arrival(sums, sums_send, sums_recv, k).wait_recv())
     total = jnp.sum(sums[...], axis=0)
     b0, b1, b2, g00, g01, g11, g02, g12 = (total[j : j + 1] for j in range(8))
     l10 = g01 / g00
@@ -282,7 +304,7 @@
     z0 = b0 / g00
     z1 = y1 / d1
 
-    for_each(1, members, lambda k: tail_copy(k).wait_recv())
+    for_each(1, members, lambda k: arrival(tail, tail_send, tail_recv, k).wait_recv())
     g22 = jnp.sum(tail[...], axis=0)
     c2 = y2 / (g22 - known)
     c1 = z1 - l21 * c2
@@ -301,15 +323,15 @@
             def _():
                 up_copy(k, j).wait_send()
 
-            for shift in range(1, pops):
-                anc_copy(k, j, shift).wait_send()
+        for shift in range(1, pops):
+            anc_copy(k, shift).wait_send()
     for k in range(2):
         for j in range(chunks):
             @pl.when(has_after)
             def _():
                 carry_copy(k, j).wait_send()
-    for_each(1, members, lambda k: sums_copy(k).wait_send())
-    for_each(1, members, lambda k: tail_copy(k).wait_send())
+    for_each(0, members - 1, lambda k: sums_copy(k).wait_send())
+    for_each(0, members - 1, lambda k: tail_copy(k).wait_send())
 
 
 def solution(mesh):
@@ -332,7 +354,7 @@
                 pltpu.SMEM(chrom_cut.shape, jnp.int32),
                 pltpu.SMEM(band_width.shape, jnp.int32),
                 pltpu.VMEM((traits, length), f32),
-                pltpu.VMEM((length // LANES, LANES, LANES), bf16),
+                pltpu.VMEM((length, length), bf16),
                 pltpu.VMEM((length, length), bf16),
                 pltpu.VMEM((length, length), bf16),
                 pltpu.VMEM((1, length), f32),
@@ -340,14 +362,14 @@
                 pltpu.VMEM((3, chunks, traits, COLS), bf16),
                 pltpu.VMEM((3, traits, length), f32),
                 pltpu.VMEM((3, chunks, traits, COLS), bf16),
-                pltpu.VMEM((3, chunks, others, traits, COLS), bf16),
+                pltpu.VMEM((3, others, chunks, traits, COLS), bf16),
                 pltpu.VMEM((2, chunks, traits, COLS), bf16),
                 pltpu.VMEM((2, chunks, traits, COLS), bf16),
                 pltpu.VMEM((members, 8, LANES), f32),
                 pltpu.VMEM((members, 1, LANES), f32),
-                dma((4 + length // LANES + 2 * chunks,)),
+                dma((4 + 2 * chunks,)),
                 dma((3, chunks)), dma((3, chunks)),
-                dma((3, chunks, others)), dma((3, chunks, others)),
+                dma((3, others)), dma((3, others)),
                 dma((2, chunks)), dma((2, chunks)),
                 dma((members,)), dma((members,)), dma((members,)), dma((members,)),
             ],

time: 25.1 us -> 24.4 us (0.972)
  Pallas kernels: 23.4 us -> 22.7 us
    pallas_call x1, Pallas kernels: 23.4 us -> 22.7 us  [body(): pl.pallas_call(functools.partial(kernel, blocks, pops), out_shape=jax.Sha...]
where the time goes in v3:
time: 24.4 us; the launch traced here: 24.3 us
  Pallas kernels  22.7 us (93%)
  local copies, waits for them, and re-layouts  1.57 us (6%)
    pallas_call x1, Pallas kernels, body(): pl.pallas_call(functools.partial(kernel, blocks, pops), out_shape=jax.Sha...  22.7 us
    unnamed x1, local copies, waits for them, and re-layouts  1.57 us

profile of v3, /device:TPU:0, one launch (start us, length us, event | category | flops | bytes accessed | tf_op | source)
XLA Modules:
  0.0 24.3 jit_solution(9414605697093079596)
XLA Ops:
  0.0 22.7 %shard_map.64 = f32[1,32,1024]{2,1,0:T(8,128)} custom-call(f32[2,2]{1,0:T(2,128)} %prior_hbm.1, s32[4]{0:T(128)} %cuts_hbm.1, s32[4]{0:T(128)} %widths_hbm.1, f32[1,32,1024]{2,1,0:T(8,128)} %z_hbm.1, bf16[1,1024,1024]{2,1,0:T(8,128)(2,1)} %diag_hbm.1, bf16[1,1024,1024]{2,1,0:T(8,128)(2,1)} %next_hbm.1), custom_call_target="tpu_custom_call" | custom-call | tf_op jit(solution)/shard_map/pallas_call | solution.py:347
  22.7 1.6 %copy.8 = f32[1,32,1024]{2,1,0:T(8,128)} copy(f32[1,32,1024]{2,1,0:T(8,128)} %shard_map.64) | data formatting | bytes 262144

commit v4 on v3

--- a/solution.py
+++ b/solution.py
@@ -218,13 +218,7 @@
             def _():
                 up_copy(k, j).wait_recv()
 
-            if k == 0:
-                part = lax.dot_general(
-                    up[k, j], nv[:, span(j)], (((1,), (1,)), ((), ())),
-                    preferred_element_type=jnp.float32,
-                )
-            else:
-                part = jnp.dot(up[k, j], tv[span(j)], preferred_element_type=jnp.float32)
+            part = jnp.dot(up[k, j], tv[span(j)], preferred_element_type=jnp.float32)
             total = part if total is None else total + part
         return total
 
@@ -249,7 +243,7 @@
         if k > 0:
             send_carry(k)
         dot_diag(k)
-        if k == 1:
+        if k == 0:
             turn_next()
         image[k] = image[k] + dot_up(k)
         for j in range(chunks):

time: 24.4 us -> 24.5 us (level)
  no operation moved by 1% of the time
where the time goes in v4:
time: 24.5 us; the launch traced here: 24.3 us
  Pallas kernels  22.7 us (93%)
  local copies, waits for them, and re-layouts  1.57 us (6%)
    pallas_call x1, Pallas kernels, body(): pl.pallas_call(functools.partial(kernel, blocks, pops), out_shape=jax.Sha...  22.7 us
    unnamed x1, local copies, waits for them, and re-layouts  1.57 us

profile of v4, /device:TPU:0, one launch (start us, length us, event | category | flops | bytes accessed | tf_op | source)
XLA Modules:
  0.0 24.3 jit_solution(10948008682031308889)
XLA Ops:
  0.0 22.7 %shard_map.64 = f32[1,32,1024]{2,1,0:T(8,128)} custom-call(f32[2,2]{1,0:T(2,128)} %prior_hbm.1, s32[4]{0:T(128)} %cuts_hbm.1, s32[4]{0:T(128)} %widths_hbm.1, f32[1,32,1024]{2,1,0:T(8,128)} %z_hbm.1, bf16[1,1024,1024]{2,1,0:T(8,128)(2,1)} %diag_hbm.1, bf16[1,1024,1024]{2,1,0:T(8,128)(2,1)} %next_hbm.1), custom_call_target="tpu_custom_call" | custom-call | tf_op jit(solution)/shard_map/pallas_call | solution.py:341
  22.8 1.6 %copy.8 = f32[1,32,1024]{2,1,0:T(8,128)} copy(f32[1,32,1024]{2,1,0:T(8,128)} %shard_map.64) | data formatting | bytes 262144
